TPU v7x, 32 devices: a whole 2x2x4 slice. The times are simulated.
32 devices in a mesh: groups: 2 (over y), sec: 2 (over x), row: 4 (over z), col: 2 (over core).
Axes of the slice: x: 2, y: 2, z: 4, core: 2. Of those that a mesh axis runs over, the one named last changes fastest.
Arguments:
- factors: bfloat16 [4, 2048, 2048], P(('groups', 'sec'), 'row', 'col'), parts along dimension 0, may hold values from -0.125 to 0.125
- inverses: bfloat16 [4, 2048, 2048], P(('groups', 'sec'), 'row', 'col'), parts along dimension 0, may hold values from -1.4 to 1.4, as said below
- sigma_end: float32 [4096, 2048], P(('groups', 'row'), 'col'), parts along dimension 0, may hold values from -1 to 6, as said below
Outputs:
- variance: float32 [4, 2048, 2048], P(('groups', 'sec'), 'row', 'col'), parts along dimension 0
There are 2 independent parts, one for each index of `groups`. A program takes and returns all parts, laid end to end along the dimension named above; each array names one. Nothing has to cross between parts.
Inputs may be any that keep to these rules, and one draw needn't show every extreme that they name: inverses[t] is lower triangular; its diagonal entries lie in 0.6 to 1.4. sigma_end is symmetric with diagonal entries in 2.5 to 6.
All inputs are finite; a program needn't handle non-finite values.
Results may differ from a plain program's by a relative error of at most 0.011.
Values may be sent and summed in bfloat16 or wider, within the bound.
A program may use at most 64 MiB of HBM per device.

v0:
```python
import jax
import jax.numpy as jnp
from jax import lax
from jax.sharding import PartitionSpec as P


def partner(shard, axis, stride):
    return lax.ppermute(shard, axis, [(i, i ^ 1 << stride) for i in range(lax.axis_size(axis))])


def passed_along(value, axis, steps):
    count = lax.axis_size(axis)
    first, last = (max(0, -steps), min(count, count - steps))
    return lax.ppermute(value, axis, [(source, source + steps) for source in range(first, last)])


def local(factors, inverses, sigma_end):
    row_size = lax.axis_size("row")
    col_size = lax.axis_size("col")
    sec_size = lax.axis_size("sec")
    row_index = lax.axis_index("row")
    col_index = lax.axis_index("col")
    sec_index = lax.axis_index("sec")
    _, tile_rows, _ = factors.shape
    per_column = row_size // col_size
    offset = row_index % per_column * tile_rows
    owns_panel = col_index == row_index // per_column

    def gather(tile):
        return lax.all_gather(tile, "row", axis=0, tiled=True)

    def left_of(full):
        mine = lax.dynamic_slice_in_dim(full, offset, tile_rows, 1)
        return jnp.where(owns_panel, mine, partner(mine, "col", 0))

    def cross(left, full):
        return lax.dot_general(
            left, full, (((0,), (0,)), ((), ())), preferred_element_type=jnp.float32
        )

    current = sigma_end.astype(jnp.bfloat16)
    factor = gather(factors[0])
    state = gather(current)
    inverse = gather(inverses[0])
    factor_left = left_of(factor)
    diagonal = cross(left_of(inverse), inverse)
    result = None
    for segment in range(sec_size):
        half = cross(factor_left, state).astype(jnp.bfloat16)
        whole = lax.all_gather(half, "col", axis=1, tiled=True)
        block = diagonal + jnp.dot(whole, factor, preferred_element_type=jnp.float32)
        active = sec_index == sec_size - 1 - segment
        result = block if result is None else jnp.where(active, block, result)
        if segment < sec_size - 1:
            state = gather(passed_along(block.astype(jnp.bfloat16), "sec", -1))
    return result[None]


def solution(mesh):
    in_specs = (
        P(("groups", "sec"), "row", "col"),
        P(("groups", "sec"), "row", "col"),
        P(("groups", "row"), "col"),
    )
    out_specs = P(("groups", "sec"), "row", "col")
    return jax.shard_map(local, mesh=mesh, in_specs=in_specs, out_specs=out_specs, check_vma=False)
```

profile of v0, /device:TPU:0, one launch (start us, length us, event | category | flops | bytes accessed | tf_op | source)
XLA Modules:
  0.0 415.6 jit_solution(8728628893357089546)
XLA Ops:
  6.5 0.7 all-gather.19.cloned.1.call-update
  7.3 0.0 all-gather.17.cloned.1.call-start
  7.3 0.7 all-gather.17.cloned.1.call-update
  8.0 0.0 all-gather.9.cloned.1.call-start
  8.1 2.8 convert_element_type.12
  10.8 0.0 all-gather.9.cloned.1.call-update
  10.8 0.0 all-gather.11.cloned.1.call-start
  10.9 81.5 %all-gather.19.cloned.1.call-done = bf16[1,2048,1024]{2,1,0:T(8,128)(2,1)} async-done(((bf16[1,512,1024]{2,1,0:T(8,128)(2,1)}), bf16[1,2048,1024]{2,1,0:T(8,128)(2,1)}) %all-gather.19.cloned.1.call-update) | async-done | bytes 4194320 | tf_op jit(solution)/shard_map/all_gather | solution.py:30
  92.4 1.7 dynamic-slice_bitcast_fusion
  94.2 0.1 collective-permute-start.1
  94.3 79.1 %all-gather.17.cloned.1.call-done = bf16[1,2048,1024]{2,1,0:T(8,128)(2,1)} async-done(((bf16[1,512,1024]{2,1,0:T(8,128)(2,1)}), bf16[1,2048,1024]{2,1,0:T(8,128)(2,1)}) %all-gather.17.cloned.1.call-update) | async-done | bytes 4194320 | tf_op jit(solution)/shard_map/all_gather | solution.py:30
  173.3 3.0 dynamic-slice_bitcast_fusion.1
  176.4 0.0 collective-permute-start
  176.4 77.9 %all-gather.9.cloned.1.call-done = bf16[2048,1024]{1,0:T(8,128)(2,1)} async-done(((bf16[512,1024]{1,0:T(8,128)(2,1)}), bf16[2048,1024]{1,0:T(8,128)(2,1)}) %all-gather.9.cloned.1.call-update) | async-done | bytes 4194320 | tf_op jit(solution)/shard_map/all_gather | solution.py:30
  254.2 0.0 collective-permute-done.1
  254.2 5.6 %convolution_convert_fusion.1 = bf16[512,1024]{1,0:T(8,128)(2,1)} fusion(bf16[2048,1024]{1,0:T(8,128)(2,1)} %all-gather.9.cloned.1.call-done, bf16[2048,512]{1,0:T(8,128)(2,1)S(1)} %dynamic-slice_bitcast_fusion, bf16[2048,512]{1,0:T(8,128)(2,1)} %collective-permute-done.1, pred[]{:T(512)S(6)} %eq.9), kind=kOutput, calls=%fused_computation.14 | convolution fusion | flops 2149056512 | bytes 9437185 | tf_op jit(solution)/shard_map/dot_general | solution.py:37
  259.8 0.0 all-gather.11.cloned.1.call-update
  259.8 0.0 all-gather.13.cloned.1.call-start
  259.8 0.0 collective-permute-done
  259.9 6.6 %fusion.4 = f32[512,1024]{1,0:T(8,128)} fusion(bf16[1,2048,1024]{2,1,0:T(8,128)(2,1)} %all-gather.17.cloned.1.call-done, bf16[2048,512]{1,0:T(8,128)(2,1)} %dynamic-slice_bitcast_fusion.1, bf16[2048,512]{1,0:T(8,128)(2,1)} %collective-permute-done, pred[]{:T(512)S(6)} %eq.9), kind=kOutput, calls=%fused_computation.4 | convolution fusion | flops 2148532224 | bytes 10485761 | tf_op jit(solution)/shard_map/dot_general | solution.py:37
  266.4 3.2 all-gather.11.cloned.1.call-done
  269.7 7.1 %fusion.13 = (bf16[512,1024]{1,0:T(8,128)(2,1)S(1)}, f32[512,1024]{1,0:T(8,128)}) fusion(f32[512,1024]{1,0:T(8,128)} %fusion.4, bf16[512,2048]{1,0:T(8,128)(2,1)} %all-gather.11.cloned.1.call-done, bf16[1,2048,1024]{2,1,0:T(8,128)(2,1)} %all-gather.19.cloned.1.call-done), kind=kOutput, calls=%fused_computation.15 | convolution fusion | flops 2148532224 | bytes 11534336 | tf_op jit(solution)/shard_map/dot_general | solution.py:51
  276.8 1.3 collective-permute-start.2
  278.1 25.9 %collective-permute-done.2 = bf16[512,1024]{1,0:T(8,128)(2,1)S(1)} collective-permute-done((bf16[512,1024]{1,0:T(8,128)(2,1)S(1)}, bf16[512,1024]{1,0:T(8,128)(2,1)S(1)}, u32[]{:S(2)}, u32[]{:S(2)}) %collective-permute-start.2) | collective-permute-done | bytes 1048608 | tf_op jit(solution)/shard_map/ppermute | solution.py:14
  304.0 1.0 copy-done
  305.0 0.0 all-gather.13.cloned.1.call-update
  305.0 0.0 all-gather.15.cloned.1.call-start
  305.0 81.2 %all-gather.13.cloned.1.call-done = bf16[2048,1024]{1,0:T(8,128)(2,1)} async-done(((bf16[512,1024]{1,0:T(8,128)(2,1)}), bf16[2048,1024]{1,0:T(8,128)(2,1)}) %all-gather.13.cloned.1.call-update) | async-done | bytes 4194320 | tf_op jit(solution)/shard_map/all_gather | solution.py:30
  386.3 5.5 %convolution_convert_fusion = bf16[512,1024]{1,0:T(8,128)(2,1)} fusion(bf16[2048,1024]{1,0:T(8,128)(2,1)} %all-gather.13.cloned.1.call-done, bf16[2048,512]{1,0:T(8,128)(2,1)S(1)} %dynamic-slice_bitcast_fusion, bf16[2048,512]{1,0:T(8,128)(2,1)} %collective-permute-done.1, pred[]{:T(512)S(6)} %eq.9), kind=kOutput, calls=%fused_computation.13 | convolution fusion | flops 2149056512 | bytes 9437185 | tf_op jit(solution)/shard_map/dot_general | solution.py:37
  391.8 0.0 all-gather.15.cloned.1.call-update
  391.8 9.9 %all-gather.15.cloned.1.call-done = bf16[512,2048]{1,0:T(8,128)(2,1)} async-done(((bf16[512,1024]{1,0:T(8,128)(2,1)}), bf16[512,2048]{1,0:T(8,128)(2,1)}) %all-gather.15.cloned.1.call-update) | async-done | bytes 2097168 | tf_op jit(solution)/shard_map/all_gather | solution.py:50
  401.7 7.1 %select_bitcast_fusion = f32[1,512,1024]{2,1,0:T(8,128)} fusion(f32[512,1024]{1,0:T(8,128)} %get-tuple-element.6, f32[512,1024]{1,0:T(8,128)} %fusion.4, bf16[512,2048]{1,0:T(8,128)(2,1)} %all-gather.15.cloned.1.call-done, bf16[1,2048,1024]{2,1,0:T(8,128)(2,1)} %all-gather.19.cloned.1.call-done, pred[]{:T(512)S(6)} %eq.8), kind=kOutput, calls=%fused_computation.8 | convolution fusion | flops 2148532224 | bytes 12582913 | tf_op jit(solution)/shard_map/dot_general | solution.py:51
  (2 shorter events, 0.0 us)
Async XLA Ops:
  6.5 85.9 %all-gather.19.cloned.1.call-start = ((), (), s32[]{:S(2)}) async-start(), calls=%async_computation.5 | async-start | bytes 5242880 | tf_op jit(solution)/shard_map/all_gather | solution.py:30
  7.3 166.1 %all-gather.17.cloned.1.call-start = ((), (), s32[]{:S(2)}) async-start(), calls=%async_computation.4 | async-start | bytes 5242880 | tf_op jit(solution)/shard_map/all_gather | solution.py:30
  8.0 246.2 %all-gather.9.cloned.1.call-start = ((), (), s32[]{:S(2)}) async-start(), calls=%async_computation | async-start | bytes 5242880 | tf_op jit(solution)/shard_map/all_gather | solution.py:30
  10.8 258.9 %all-gather.11.cloned.1.call-start = ((), (), s32[]{:S(2)}) async-start(), calls=%async_computation.1 | async-start | bytes 3145728 | tf_op jit(solution)/shard_map/all_gather | solution.py:50
  94.2 160.1 %collective-permute-start.1 = (bf16[2048,512]{1,0:T(8,128)(2,1)S(1)}, bf16[2048,512]{1,0:T(8,128)(2,1)}, u32[]{:S(2)}, u32[]{:S(2)}) collective-permute-start(bf16[2048,512]{1,0:T(8,128)(2,1)S(1)} %dynamic-slice_bitcast_fusion), channel_id=1, source_target_pairs={{0,1},{1,0},{2,3},{3,2},{4,5},{5,4},{6,7},{7,6},{8,9},{9,8},{10,11... | collective-permute-start | bytes 6291464 | tf_op jit(solution)/shard_map/ppermute | solution.py:8
  176.4 83.5 %collective-permute-start = (bf16[2048,512]{1,0:T(8,128)(2,1)}, bf16[2048,512]{1,0:T(8,128)(2,1)}, u32[]{:S(2)}, u32[]{:S(2)}) collective-permute-start(bf16[2048,512]{1,0:T(8,128)(2,1)} %dynamic-slice_bitcast_fusion.1), channel_id=1, source_target_pairs={{0,1},{1,0},{2,3},{3,2},{4,5},{5,4},{6,7},{7,6},{8,9},{9,8},{10,11... | collective-permute-start | bytes 6291464 | tf_op jit(solution)/shard_map/ppermute | solution.py:8
  259.8 126.5 %all-gather.13.cloned.1.call-start = ((), (), s32[]{:S(2)}) async-start(), calls=%async_computation.2 | async-start | bytes 5242880 | tf_op jit(solution)/shard_map/all_gather | solution.py:30
  276.8 27.2 %collective-permute-start.2 = (bf16[512,1024]{1,0:T(8,128)(2,1)S(1)}, bf16[512,1024]{1,0:T(8,128)(2,1)S(1)}, u32[]{:S(2)}, u32[]{:S(2)}) collective-permute-start(bf16[512,1024]{1,0:T(8,128)(2,1)S(1)} %get-tuple-element.5), channel_id=1, source_target_pairs={{8,0},{9,1},{10,2},{11,3},{12,4},{13,5},{14,6},{15,7},{24,16},{25,... | collective-permute-start | bytes 3145736 | tf_op jit(solution)/shard_map/ppermute | solution.py:14
  304.0 1.0 copy-start
  305.0 96.7 %all-gather.15.cloned.1.call-start = ((), (), s32[]{:S(2)}) async-start(), calls=%async_computation.3 | async-start | bytes 3145728 | tf_op jit(solution)/shard_map/all_gather | solution.py:50
Sparse Core Ops, SparseCore 0:
  8.9 83.4 all-gather.18
  94.0 79.2 all-gather.16
  174.9 79.2 all-gather.8
  259.9 9.7 all-gather.10
  305.1 81.1 all-gather.12
  391.9 9.7 all-gather.14
where the time goes:
time: 416 us
  waiting for transfers between devices  360 us (87%)
  matrix products  31.9 us (8%)
  between operations  13.5 us (3%)
  local copies, waits for them, and re-layouts  5.75 us (1%)
    all_gather x4, waiting for transfers between devices, gather(): return lax.all_gather(tile, 'row', axis=0, tiled=True)  320 us
    ppermute x1, waiting for transfers between devices, passed_along(): lax.ppermute(value, axis, [(source, source + steps) for source in range(f...  25.9 us
    dot_general x3, matrix products, cross(): lax.dot_general(left, full, (((0,), (0,)), ((), ())), preferred_element_t...  17.7 us
    dot_general x2, matrix products, local(): jnp.dot(whole, factor, preferred_element_type=jnp.float32)  14.2 us
    all_gather x2, waiting for transfers between devices, local(): whole = lax.all_gather(half, 'col', axis=1, tiled=True)  13.1 us
  transfers between devices with their start and end apart: 9, of which 7 were waited for; matrix products, arithmetic and copies ran while one was open for 5% of the time, Pallas kernels for 0%

commit v1 on v0

--- a/solution.py
+++ b/solution.py
@@ -1,7 +1,25 @@
+import functools
 import jax
 import jax.numpy as jnp
 from jax import lax
 from jax.sharding import PartitionSpec as P
+
+
+def _draw_rates(raw, in_dim):
+    w_next = lax.psum(1, "row")
+    block_now = lax.axis_index("row")
+    next_value, y2 = (w_next, block_now)
+    field_out, oldest = (raw, 1)
+    while oldest < next_value:
+        odd = lax.ppermute(field_out, "row", [(k0, k0 ^ oldest) for k0 in range(next_value)])
+        fresh = jnp.concatenate([field_out, odd], axis=in_dim)
+        t1 = jnp.concatenate([odd, field_out], axis=in_dim)
+        field_out = jnp.where(y2 & oldest == 0, fresh, t1)
+        oldest = 2 * oldest
+    return field_out
+
+
+switch_desk = functools.partial(_draw_rates, in_dim=0)
 
 
 def partner(shard, axis, stride):
@@ -27,7 +45,7 @@
     owns_panel = col_index == row_index // per_column
 
     def gather(tile):
-        return lax.all_gather(tile, "row", axis=0, tiled=True)
+        return switch_desk(tile)
 
     def left_of(full):
         mine = lax.dynamic_slice_in_dim(full, offset, tile_rows, 1)

time: 416 us -> 510 us (1.23)
  waiting for transfers between devices: 360 us -> 421 us
  other arithmetic: 2.75 us -> 20.1 us
  starting transfers between devices: 1.56 us -> 18.8 us
    ppermute x0 -> x8, waiting for transfers between devices: none -> 377 us  [_draw_rates(): lax.ppermute(field_out, 'row', [(k0, k0 ^ oldest) for k0 in range(next_va...]
    all_gather x4 -> x0, waiting for transfers between devices: 320 us -> none  [gather(): return lax.all_gather(tile, 'row', axis=0, tiled=True)]
    select_n x0 -> x6, other arithmetic: none -> 19.9 us  [_draw_rates(): field_out = jnp.where(y2 & oldest == 0, fresh, t1)]
    ppermute x0 -> x8, starting transfers between devices: none -> 17.3 us  [_draw_rates(): lax.ppermute(field_out, 'row', [(k0, k0 ^ oldest) for k0 in range(next_va...]
  transfers between devices with their start and end apart: 9 -> 13, of which waited for: 7 -> 11; matrix products, arithmetic and copies ran while one was open for 5% -> 6% of each run, Pallas kernels for 0% -> 0%
where the time goes in v1:
time: 510 us; the launch traced here: 509 us
  waiting for transfers between devices  421 us (83%)
  matrix products  31.3 us (6%)
  other arithmetic  20.1 us (4%)
  starting transfers between devices  18.8 us (4%)
  between operations  13.5 us (3%)
    ppermute x8, waiting for transfers between devices, _draw_rates(): lax.ppermute(field_out, 'row', [(k0, k0 ^ oldest) for k0 in range(next_va...  377 us
    ppermute x1, waiting for transfers between devices, passed_along(): lax.ppermute(value, axis, [(source, source + steps) for source in range(f...  25.9 us
    select_n x6, other arithmetic, _draw_rates(): field_out = jnp.where(y2 & oldest == 0, fresh, t1)  19.9 us
    all_gather x2, waiting for transfers between devices, local(): whole = lax.all_gather(half, 'col', axis=1, tiled=True)  17.8 us
    ppermute x8, starting transfers between devices, _draw_rates(): lax.ppermute(field_out, 'row', [(k0, k0 ^ oldest) for k0 in range(next_va...  17.3 us
    dot_general x3, matrix products, cross(): lax.dot_general(left, full, (((0,), (0,)), ((), ())), preferred_element_t...  17.1 us
    dot_general x2, matrix products, local(): jnp.dot(whole, factor, preferred_element_type=jnp.float32)  14.2 us
  transfers between devices with their start and end apart: 13, of which 11 were waited for; matrix products, arithmetic and copies ran while one was open for 6% of the time, Pallas kernels for 0%

profile of v1, /device:TPU:0, one launch (start us, length us, event | category | flops | bytes accessed | tf_op | source)
XLA Modules:
  0.0 509.4 jit_solution(18293130368099282647)
XLA Ops:
  6.5 3.0 collective-permute-start.3
  9.6 23.4 %collective-permute-done.3 = bf16[512,1024]{1,0:T(8,128)(2,1)S(1)} collective-permute-done((bf16[512,1024]{1,0:T(8,128)(2,1)}, bf16[512,1024]{1,0:T(8,128)(2,1)S(1)}, u32[]{:S(2)}, u32[]{:S(2)}) %collective-permute-start.3) | collective-permute-done | bytes 1048608 | tf_op jit(solution)/shard_map/ppermute | solution.py:14
  32.9 2.7 maximum_select_fusion.7
  35.6 2.8 collective-permute-start.4
  38.5 1.6 collective-permute-start
  40.7 66.4 %collective-permute-done = bf16[512,1024]{1,0:T(8,128)(2,1)} collective-permute-done((bf16[512,1024]{1,0:T(8,128)(2,1)}, bf16[512,1024]{1,0:T(8,128)(2,1)}, u32[]{:S(2)}, u32[]{:S(2)}) %collective-permute-start) | collective-permute-done | bytes 1048608 | tf_op jit(solution)/shard_map/ppermute | solution.py:14
  107.1 4.7 maximum_select_fusion.6
  111.8 2.4 collective-permute-start.1
  114.1 15.3 %collective-permute-done.6 = bf16[512,1024]{1,0:T(8,128)(2,1)} collective-permute-done((bf16[512,1024]{1,0:T(8,128)(2,1)S(1)}, bf16[512,1024]{1,0:T(8,128)(2,1)}, u32[]{:S(2)}, u32[]{:S(2)}) %collective-permute-start.6) | collective-permute-done | bytes 1048608 | tf_op jit(solution)/shard_map/ppermute | solution.py:14
  129.5 3.9 maximum_select_fusion.8
  133.3 2.5 collective-permute-start.7
  135.8 83.6 %collective-permute-done.4 = bf16[1024,1024]{1,0:T(8,128)(2,1)} collective-permute-done((bf16[1024,1024]{1,0:T(8,128)(2,1)S(1)}, bf16[1024,1024]{1,0:T(8,128)(2,1)}, u32[]{:S(2)}, u32[]{:S(2)}) %collective-permute-start.4) | collective-permute-done | bytes 2097184 | tf_op jit(solution)/shard_map/ppermute | solution.py:14
  219.4 3.5 maximum_select_fusion.1
  223.2 1.7 copy-done
  224.9 39.5 %collective-permute-done.1 = bf16[1024,1024]{1,0:T(8,128)(2,1)} collective-permute-done((bf16[1024,1024]{1,0:T(8,128)(2,1)}, bf16[1024,1024]{1,0:T(8,128)(2,1)}, u32[]{:S(2)}, u32[]{:S(2)}) %collective-permute-start.1) | collective-permute-done | bytes 2097184 | tf_op jit(solution)/shard_map/ppermute | solution.py:14
  264.4 4.2 maximum_select_fusion
  268.6 1.7 constant_dynamic-slice_fusion.1
  271.2 37.1 %collective-permute-done.7 = bf16[1024,1024]{1,0:T(8,128)(2,1)} collective-permute-done((bf16[1024,1024]{1,0:T(8,128)(2,1)}, bf16[1024,1024]{1,0:T(8,128)(2,1)}, u32[]{:S(2)}, u32[]{:S(2)}) %collective-permute-start.7) | collective-permute-done | bytes 2097184 | tf_op jit(solution)/shard_map/ppermute | solution.py:14
  308.3 7.0 %fusion.18 = bf16[512,1024]{1,0:T(8,128)(2,1)} fusion(bf16[1024,1024]{1,0:T(8,128)(2,1)} %collective-permute-done.7, bf16[1024,1024]{1,0:T(8,128)(2,1)} %maximum_select_fusion.8, pred[]{:T(512)S(6)} %eq.22, bf16[2048,512]{1,0:T(8,128)(2,1)S(1)} %constant_dynamic-slice_fusion, bf16[2048,512]{1,0:T(8,128)(2,1)} %collective-permute-done.5, pred[]{:T(512)S(6)} %eq.11), kind=kOutput, calls=%fused_computation.29 | convolution fusion | flops 2167930880 | bytes 9437186 | tf_op jit(solution)/shard_map/dot_general | solution.py:55
  315.6 6.5 %fusion.14 = f32[512,1024]{1,0:T(8,128)} fusion(bf16[2048,1024]{1,0:T(8,128)(2,1)} %copy-done.1, bf16[2048,512]{1,0:T(8,128)(2,1)} %constant_dynamic-slice_fusion.1, bf16[2048,512]{1,0:T(8,128)(2,1)} %collective-permute-done.2, pred[]{:T(512)S(6)} %eq.11), kind=kOutput, calls=%fused_computation.23 | convolution fusion | flops 2148532224 | bytes 10485761 | tf_op jit(solution)/shard_map/dot_general | solution.py:55
  322.1 5.3 %all-gather.3.cloned.1.call-done = bf16[512,2048]{1,0:T(8,128)(2,1)} async-done(((bf16[512,1024]{1,0:T(8,128)(2,1)}), bf16[512,2048]{1,0:T(8,128)(2,1)}) %all-gather.3.cloned.1.call-update) | async-done | bytes 2097168 | tf_op jit(solution)/shard_map/all_gather | solution.py:68
  327.4 7.1 %fusion.21 = (bf16[512,1024]{1,0:T(8,128)(2,1)S(1)}, f32[512,1024]{1,0:T(8,128)}) fusion(f32[512,1024]{1,0:T(8,128)} %fusion.14, bf16[512,2048]{1,0:T(8,128)(2,1)} %all-gather.3.cloned.1.call-done, bf16[2048,1024]{1,0:T(8,128)(2,1)} %copy-done), kind=kOutput, calls=%fused_computation.34 | convolution fusion | flops 2148532224 | bytes 11534336 | tf_op jit(solution)/shard_map/dot_general | solution.py:69
  334.6 1.3 collective-permute-start.8
  335.8 25.9 %collective-permute-done.8 = bf16[512,1024]{1,0:T(8,128)(2,1)S(1)} collective-permute-done((bf16[512,1024]{1,0:T(8,128)(2,1)S(1)}, bf16[512,1024]{1,0:T(8,128)(2,1)S(1)}, u32[]{:S(2)}, u32[]{:S(2)}) %collective-permute-start.8) | collective-permute-done | bytes 1048608 | tf_op jit(solution)/shard_map/ppermute | solution.py:32
  361.7 1.8 collective-permute-start.9
  363.5 22.8 %collective-permute-done.9 = bf16[512,1024]{1,0:T(8,128)(2,1)S(1)} collective-permute-done((bf16[512,1024]{1,0:T(8,128)(2,1)S(1)}, bf16[512,1024]{1,0:T(8,128)(2,1)S(1)}, u32[]{:S(2)}, u32[]{:S(2)}) %collective-permute-start.9) | collective-permute-done | bytes 1048608 | tf_op jit(solution)/shard_map/ppermute | solution.py:14
  386.4 1.0 maximum_select_fusion.9
  387.4 2.7 collective-permute-start.10
  390.1 89.4 %collective-permute-done.10 = bf16[1024,1024]{1,0:T(8,128)(2,1)S(1)} collective-permute-done((bf16[1024,1024]{1,0:T(8,128)(2,1)S(1)}, bf16[1024,1024]{1,0:T(8,128)(2,1)S(1)}, u32[]{:S(2)}, u32[]{:S(2)}) %collective-permute-start.10) | collective-permute-done | bytes 2097184 | tf_op jit(solution)/shard_map/ppermute | solution.py:14
  479.5 3.5 fusion.17
  483.0 12.5 %all-gather.5.cloned.1.call-done = bf16[512,2048]{1,0:T(8,128)(2,1)} async-done(((bf16[512,1024]{1,0:T(8,128)(2,1)}), bf16[512,2048]{1,0:T(8,128)(2,1)}) %all-gather.5.cloned.1.call-update) | async-done | bytes 2097168 | tf_op jit(solution)/shard_map/all_gather | solution.py:68
  495.5 7.1 %select_bitcast_fusion = f32[1,512,1024]{2,1,0:T(8,128)} fusion(f32[512,1024]{1,0:T(8,128)} %get-tuple-element.6, f32[512,1024]{1,0:T(8,128)} %fusion.14, bf16[512,2048]{1,0:T(8,128)(2,1)} %all-gather.5.cloned.1.call-done, bf16[2048,1024]{1,0:T(8,128)(2,1)} %copy-done, pred[]{:T(512)S(6)} %eq.10), kind=kOutput, calls=%fused_computation.22 | convolution fusion | flops 2148532224 | bytes 12582913 | tf_op jit(solution)/shard_map/dot_general | solution.py:69
  (16 shorter events, 2.1 us)
Async XLA Ops:
  6.5 320.9 %all-gather.3.cloned.1.call-start = ((), (), s32[]{:S(2)}) async-start(), calls=%async_computation | async-start | bytes 3145728 | tf_op jit(solution)/shard_map/all_gather | solution.py:68
  6.5 26.4 %collective-permute-start.3 = (bf16[512,1024]{1,0:T(8,128)(2,1)}, bf16[512,1024]{1,0:T(8,128)(2,1)S(1)}, u32[]{:S(2)}, u32[]{:S(2)}) collective-permute-start(bf16[512,1024]{1,0:T(8,128)(2,1)} %bitcast.9), channel_id=1, source_target_pairs={{0,2},{2,0},{4,6},{6,4},{1,3},{3,1},{5,7},{7,5},{8,10},{10,8},{12,... | collective-permute-start | bytes 3145736 | tf_op jit(solution)/shard_map/ppermute | solution.py:14
  9.6 30.5 %copy-start.2 = (f32[512,1024]{1,0:T(8,128)S(1)}, f32[512,1024]{1,0:T(8,128)}, u32[]{:S(2)}) copy-start(f32[512,1024]{1,0:T(8,128)} %param.5) | copy-start | bytes 6291460
  35.6 183.8 %collective-permute-start.4 = (bf16[1024,1024]{1,0:T(8,128)(2,1)S(1)}, bf16[1024,1024]{1,0:T(8,128)(2,1)}, u32[]{:S(2)}, u32[]{:S(2)}) collective-permute-start(bf16[1024,1024]{1,0:T(8,128)(2,1)S(1)} %maximum_select_fusion.7), channel_id=1, source_target_pairs={{0,4},{2,6},{4,0},{6,2},{1,5},{3,7},{5,1},{7,3},{8,12},{10,14},{12... | collective-permute-start | bytes 6291464 | tf_op jit(solution)/shard_map/ppermute | solution.py:14
  38.5 68.7 %collective-permute-start = (bf16[512,1024]{1,0:T(8,128)(2,1)}, bf16[512,1024]{1,0:T(8,128)(2,1)}, u32[]{:S(2)}, u32[]{:S(2)}) collective-permute-start(bf16[512,1024]{1,0:T(8,128)(2,1)} %bitcast), channel_id=1, source_target_pairs={{0,2},{2,0},{4,6},{6,4},{1,3},{3,1},{5,7},{7,5},{8,10},{10,8},{12,... | collective-permute-start | bytes 3145736 | tf_op jit(solution)/shard_map/ppermute | solution.py:14
  40.2 89.3 %collective-permute-start.6 = (bf16[512,1024]{1,0:T(8,128)(2,1)S(1)}, bf16[512,1024]{1,0:T(8,128)(2,1)}, u32[]{:S(2)}, u32[]{:S(2)}) collective-permute-start(bf16[512,1024]{1,0:T(8,128)(2,1)S(1)} %convert_element_type.12), channel_id=1, source_target_pairs={{0,2},{2,0},{4,6},{6,4},{1,3},{3,1},{5,7},{7,5},{8,10},{10,8},{12,... | collective-permute-start | bytes 3145736 | tf_op jit(solution)/shard_map/ppermute | solution.py:14
  111.8 152.6 %collective-permute-start.1 = (bf16[1024,1024]{1,0:T(8,128)(2,1)}, bf16[1024,1024]{1,0:T(8,128)(2,1)}, u32[]{:S(2)}, u32[]{:S(2)}) collective-permute-start(bf16[1024,1024]{1,0:T(8,128)(2,1)} %maximum_select_fusion.6), channel_id=1, source_target_pairs={{0,4},{2,6},{4,0},{6,2},{1,5},{3,7},{5,1},{7,3},{8,12},{10,14},{12... | collective-permute-start | bytes 6291464 | tf_op jit(solution)/shard_map/ppermute | solution.py:14
  133.3 174.9 %collective-permute-start.7 = (bf16[1024,1024]{1,0:T(8,128)(2,1)}, bf16[1024,1024]{1,0:T(8,128)(2,1)}, u32[]{:S(2)}, u32[]{:S(2)}) collective-permute-start(bf16[1024,1024]{1,0:T(8,128)(2,1)} %maximum_select_fusion.8), channel_id=1, source_target_pairs={{0,4},{2,6},{4,0},{6,2},{1,5},{3,7},{5,1},{7,3},{8,12},{10,14},{12... | collective-permute-start | bytes 6291464 | tf_op jit(solution)/shard_map/ppermute | solution.py:14
  222.9 1.9 copy-start
  224.9 83.4 %collective-permute-start.5 = (bf16[2048,512]{1,0:T(8,128)(2,1)S(1)}, bf16[2048,512]{1,0:T(8,128)(2,1)}, u32[]{:S(2)}, u32[]{:S(2)}) collective-permute-start(bf16[2048,512]{1,0:T(8,128)(2,1)S(1)} %constant_dynamic-slice_fusion), channel_id=1, source_target_pairs={{0,1},{1,0},{2,3},{3,2},{4,5},{5,4},{6,7},{7,6},{8,9},{9,8},{10,11... | collective-permute-start | bytes 6291464 | tf_op jit(solution)/shard_map/ppermute | solution.py:26
  268.6 2.6 copy-start.1
  271.2 44.4 %collective-permute-start.2 = (bf16[2048,512]{1,0:T(8,128)(2,1)}, bf16[2048,512]{1,0:T(8,128)(2,1)}, u32[]{:S(2)}, u32[]{:S(2)}) collective-permute-start(bf16[2048,512]{1,0:T(8,128)(2,1)} %constant_dynamic-slice_fusion.1), channel_id=1, source_target_pairs={{0,1},{1,0},{2,3},{3,2},{4,5},{5,4},{6,7},{7,6},{8,9},{9,8},{10,11... | collective-permute-start | bytes 6291464 | tf_op jit(solution)/shard_map/ppermute | solution.py:26
  315.3 180.1 %all-gather.5.cloned.1.call-start = ((), (), s32[]{:S(2)}) async-start(), calls=%async_computation.1 | async-start | bytes 3145728 | tf_op jit(solution)/shard_map/all_gather | solution.py:68
  334.6 27.2 %collective-permute-start.8 = (bf16[512,1024]{1,0:T(8,128)(2,1)S(1)}, bf16[512,1024]{1,0:T(8,128)(2,1)S(1)}, u32[]{:S(2)}, u32[]{:S(2)}) collective-permute-start(bf16[512,1024]{1,0:T(8,128)(2,1)S(1)} %get-tuple-element.5), channel_id=1, source_target_pairs={{8,0},{9,1},{10,2},{11,3},{12,4},{13,5},{14,6},{15,7},{24,16},{25,... | collective-permute-start | bytes 3145736 | tf_op jit(solution)/shard_map/ppermute | solution.py:32
  361.7 24.6 %collective-permute-start.9 = (bf16[512,1024]{1,0:T(8,128)(2,1)S(1)}, bf16[512,1024]{1,0:T(8,128)(2,1)S(1)}, u32[]{:S(2)}, u32[]{:S(2)}) collective-permute-start(bf16[512,1024]{1,0:T(8,128)(2,1)S(1)} %collective-permute-done.8), channel_id=1, source_target_pairs={{0,2},{2,0},{4,6},{6,4},{1,3},{3,1},{5,7},{7,5},{8,10},{10,8},{12,... | collective-permute-start | bytes 3145736 | tf_op jit(solution)/shard_map/ppermute | solution.py:14
  387.4 92.1 %collective-permute-start.10 = (bf16[1024,1024]{1,0:T(8,128)(2,1)S(1)}, bf16[1024,1024]{1,0:T(8,128)(2,1)S(1)}, u32[]{:S(2)}, u32[]{:S(2)}) collective-permute-start(bf16[1024,1024]{1,0:T(8,128)(2,1)S(1)} %maximum_select_fusion.9), channel_id=1, source_target_pairs={{0,4},{2,6},{4,0},{6,2},{1,5},{3,7},{5,1},{7,3},{8,12},{10,14},{12... | collective-permute-start | bytes 6291464 | tf_op jit(solution)/shard_map/ppermute | solution.py:14
Sparse Core Ops, SparseCore 0:
  315.5 11.9 all-gather.2
  483.1 12.2 all-gather.4
